TPU v7x, 32 devices: a whole 2x2x4 slice. The times are simulated.
32 devices in a mesh: dp: 4 (over x, core), expert: 8 (over z, y).
Axes of the slice: x: 2, y: 2, z: 4, core: 2. Of those that a mesh axis runs over, the one named last changes fastest.
Arguments:
- tokens: bfloat16 [4096, 2048], P(('dp', 'expert')), may hold values from -6 to 6
- expert_ids: int32 [4096, 4], P(('dp', 'expert')), may hold values from 0 to 15, all different within a row; in each aligned block of 128 rows (0 to 127, 128 to 255, ...) at most 48 rows name the same one
- gate_weights: float32 [4096, 4], P(('dp', 'expert')), may hold values from 0.05 to 0.6
- grad_out: bfloat16 [4096, 2048], P(('dp', 'expert')), may hold values from -6 to 6
- w_gate: bfloat16 [16, 2048, 384], P('expert'), may hold values from -0.125 to 0.125
- w_up: bfloat16 [16, 2048, 384], P('expert'), may hold values from -0.125 to 0.125
- w_down: bfloat16 [16, 384, 2048], P('expert'), may hold values from -0.3125 to 0.3125
Outputs:
- mixed_out: bfloat16 [4096, 2048], P(('dp', 'expert'))
- d_tokens: bfloat16 [4096, 2048], P(('dp', 'expert'))
- d_gates: float32 [4096, 4], P(('dp', 'expert'))
- d_w_gate: bfloat16 [16, 2048, 384], P('expert', 'dp')
- d_w_up: bfloat16 [16, 2048, 384], P('expert', 'dp')
- d_w_down: bfloat16 [16, 384, 2048], P('expert', None, 'dp')
Inputs may be any that keep to these rules, and one draw needn't show every extreme that they name: `expert_ids`: each row names 4 different experts; in the 128 rows of one device no expert is named more than 48 times, and in every draw some expert is named exactly 48 times by the rows of some device.
All inputs are finite; a program needn't handle non-finite values.
Results may differ from a plain program's by a relative error of at most 0.009.
Values may be sent and summed in bfloat16 or wider, within the bound.
A program may use at most 128 MiB of HBM per device.

v0:
```python
import functools

import jax
import jax.numpy as jnp
from jax import lax
from jax.experimental import pallas as pl
from jax.experimental.pallas import tpu as pltpu
from jax.sharding import PartitionSpec as P

BF16 = jnp.bfloat16
F32 = jnp.float32
MESH = pl.DeviceIdType.MESH
NN = (((1,), (0,)), ((), ()))
NT = (((1,), (1,)), ((), ()))
TN = (((0,), (0,)), ((), ()))


def dot(spec, a, b):
    return jnp.einsum(spec, a, b, preferred_element_type=F32)


def mm(a, b, dims):
    return lax.dot_general(a, b, dims, preferred_element_type=F32)


def local_wide(tokens, expert_ids, gate_weights, grad_out, w_gate, w_up, w_down):
    tok_dev, model_dim = tokens.shape
    exp_dev = w_gate.shape[0]
    owners = lax.axis_size("expert")
    experts = exp_dev * owners
    chosen = expert_ids[:, :, None] == jnp.arange(experts, dtype=jnp.int32)
    gate_of = jnp.sum(jnp.where(chosen, gate_weights[:, :, None], 0.0), axis=1)
    gates = lax.all_to_all(
        gate_of.reshape(tok_dev, owners, exp_dev).transpose(1, 2, 0), "expert", 0, 0, tiled=True
    )
    gates = gates.transpose(1, 0, 2).reshape(exp_dev, owners * tok_dev, 1)
    rows = lax.all_gather(tokens, "expert", axis=0, tiled=True)
    grads = lax.all_gather(grad_out, "expert", axis=0, tiled=True)
    gate_pre = dot("td,edf->etf", rows, w_gate)
    up_pre = dot("td,edf->etf", rows, w_up)
    d_mid = dot("td,efd->etf", grads, w_down)
    sigma = jax.nn.sigmoid(gate_pre)
    hidden = gate_pre * sigma * up_pre
    d_gate_sum = jnp.sum(hidden * d_mid, axis=2)
    d_hidden = gates * d_mid
    scaled_hidden = (gates * hidden).astype(BF16)
    d_up = (d_hidden * gate_pre * sigma).astype(BF16)
    d_gate = (d_hidden * up_pre * sigma * (1.0 + gate_pre * (1.0 - sigma))).astype(BF16)
    mixed = dot("etf,efd->td", scaled_hidden, w_down).astype(BF16)
    mixed_out = lax.psum_scatter(mixed, "expert", scatter_dimension=0, tiled=True)
    d_rows = (dot("etf,edf->td", d_gate, w_gate) + dot("etf,edf->td", d_up, w_up)).astype(BF16)
    d_tokens = lax.psum_scatter(d_rows, "expert", scatter_dimension=0, tiled=True)
    back = lax.all_to_all(
        d_gate_sum.reshape(exp_dev, owners, tok_dev).transpose(1, 0, 2), "expert", 0, 0, tiled=True
    )
    back = back.reshape(experts, tok_dev).T
    d_gates = jnp.sum(jnp.where(chosen, back[:, None, :], 0.0), axis=2)
    part_gate = dot("td,etf->edf", rows, d_gate).astype(BF16)
    part_up = dot("td,etf->edf", rows, d_up).astype(BF16)
    part_down = dot("etf,td->efd", scaled_hidden, grads).astype(BF16)
    grad_gate = lax.psum_scatter(part_gate, "dp", scatter_dimension=1, tiled=True)
    grad_up = lax.psum_scatter(part_up, "dp", scatter_dimension=1, tiled=True)
    grad_down = lax.psum_scatter(part_down, "dp", scatter_dimension=2, tiled=True)
    return (mixed_out, d_tokens, d_gates, grad_gate, grad_up, grad_down)


def slot_of(step):
    if step == 0:
        return 0
    if abs(step) == 4:
        return 1
    return 2 * step if step > 0 else 1 - 2 * step


def step_of(slot):
    if slot == 0:
        return 0
    if slot == 1:
        return 4
    return slot // 2 if slot % 2 == 0 else -(slot // 2)


RETURN_LEFT = (("m", 4), ("r", 3), ("m", 3), ("r", 2), ("m", 2), ("r", 1), ("m", 1))
RETURN_RIGHT = (("r", 4), ("m", -3), ("r", -3), ("m", -2), ("r", -2), ("m", -1), ("r", -1))


def layer_kernel(
    tok_in, grad_in, wg_in, wu_in, wd_in, ids_ref, gw_ref,
    mixed_ref, dtok_ref, dgates_ref, ogate_ref, oup_ref, odown_ref,
    x_all, g_all, wg, wu, wd, parts_m, parts_r, dgu, mid, dwgu, dwd, landed,
    pr_gu, pr_d, xr_gu, xr_d, gsend, grecv, wcol, dcol, dsend, back,
    local_sem, ag_send, ag_recv, rs_send, rs_recv, small_send, small_recv, dp_send, dp_recv,
):
    n = 8
    tok, model = tok_in.shape
    exp_dev, ff = wg.shape[0], wg.shape[2]
    half = tok // 2
    quarter = model // 4
    me = lax.axis_index("expert")
    dp = lax.axis_index("dp")
    odd = me % 2
    pos = (me // 2) * (1 - odd) + (n - 1 - me // 2) * odd

    def device_at(q):
        q = (q + 2 * n) % n
        far = q // (n // 2)
        return far * (2 * n - 1 - 2 * q) + (1 - far) * 2 * q

    right, left = device_at(pos + 1), device_at(pos - 1)
    core = dp % 2
    xpos = dp // 2
    partner = xpos * 2 + 1 - core
    across = (1 - xpos) * 2 + core
    sides = (right, left)

    barrier = pltpu.get_barrier_semaphore()
    for k in range(1, n):
        pl.semaphore_signal(
            barrier, inc=1, device_id={"expert": device_at(pos + k)}, device_id_type=MESH
        )
    for other in (partner, across):
        pl.semaphore_signal(barrier, inc=1, device_id={"dp": other}, device_id_type=MESH)

    locals_ = [
        pltpu.make_async_copy(tok_in, x_all.at[pl.ds(0, tok)], local_sem.at[0]),
        pltpu.make_async_copy(grad_in, g_all.at[pl.ds(0, tok)], local_sem.at[1]),
        pltpu.make_async_copy(wg_in, wg, local_sem.at[2]),
        pltpu.make_async_copy(wu_in, wu, local_sem.at[3]),
        pltpu.make_async_copy(wd_in, wd, local_sem.at[4]),
    ]
    for copy in locals_:
        copy.start()
    pl.semaphore_wait(barrier, n + 1)

    def send_to(src, dst, side, index):
        return pltpu.make_async_remote_copy(
            src_ref=src, dst_ref=dst,
            send_sem=ag_send.at[side, index], recv_sem=ag_recv.at[side, index],
            device_id={"expert": sides[side]}, device_id_type=MESH,
        )

    def early(side, index):
        hop, part = index // 2, index % 2
        sign = 1 if side == 0 else -1
        buf, own = ((x_all, tok_in), (g_all, grad_in))[side]
        dst = buf.at[pl.ds(slot_of(sign * (hop + 1)) * tok + part * half, half)]
        if hop == 0:
            src = own.at[pl.ds(part * half, half)]
        else:
            src = buf.at[pl.ds(slot_of(sign * hop) * tok + part * half, half)]
        return send_to(src, dst, side, index)

    def late(side, hop, part):
        if side == 0:
            buf, s, d = g_all, 2 * hop, 2 * hop + 2
        else:
            buf, s, d = x_all, 2 * hop + (hop + 2) // 3, 2 * hop + 3
        return send_to(
            buf.at[pl.ds(s * tok + part * half, half)],
            buf.at[pl.ds(d * tok + part * half, half)],
            side, 8 + 2 * hop + part,
        )

    for part in range(2):
        for side in range(2):
            early(side, part).start()

    lane = lax.broadcasted_iota(jnp.int32, (tok, 128), 1)
    expert_of_lane = jnp.where(lane % 8 < exp_dev, (lane // 8) * exp_dev + lane % 8, -1)
    gates = jnp.zeros((tok, 128), F32)
    for k in range(ids_ref.shape[1]):
        gates = gates + jnp.where(ids_ref[:, k : k + 1] == expert_of_lane, gw_ref[:, k : k + 1], 0.0)
    gsend[...] = jnp.transpose(gates)[: n * 8].reshape(n, 8, 128)

    def gate_copy(k):
        slot = slot_of(k if k <= 4 else k - 8)
        to = device_at(pos + k)
        return pltpu.make_async_remote_copy(
            src_ref=gsend.at[to], dst_ref=grecv.at[slot],
            send_sem=small_send.at[0, slot], recv_sem=small_recv.at[0, slot],
            device_id={"expert": to}, device_id_type=MESH,
        )

    for k in range(1, n):
        gate_copy(k).start()
    grecv[0] = gsend[me]
    locals_[0].wait()
    locals_[1].wait()

    for index in range(8):
        for side in range(2):
            early(side, index).wait_recv()
            if index < 6:
                early(side, index + 2).start()
            else:
                late(side, 0, index - 6).start()
        if index == 1:
            for k in range(1, n):
                gate_copy(k).wait_recv()
            cols = jnp.concatenate(
                [grecv[...].reshape(n * 8, 128), jnp.zeros((128 - n * 8, 128), F32)], axis=0
            )
            cols = jnp.transpose(cols)
            for slot in range(n):
                for e in range(exp_dev):
                    at = slot * 8 + e
                    wcol[e, pl.ds(slot * tok, tok), :] = jnp.broadcast_to(
                        cols[:, at : at + 1], (tok, 128)
                    )
        if index == 3:
            for copy in locals_[2:]:
                copy.wait()

    bufs = {"m": parts_m, "r": parts_r}
    orders = (RETURN_RIGHT, RETURN_LEFT)

    def back_copy(side, index):
        kind, step = orders[side][index]
        return pltpu.make_async_remote_copy(
            src_ref=bufs[kind].at[pl.ds(slot_of(step) * tok, tok)], dst_ref=landed.at[side, index],
            send_sem=rs_send.at[side, index], recv_sem=rs_recv.at[side, index],
            device_id={"expert": sides[side]}, device_id_type=MESH,
        )

    def stage_one(j):
        rows = pl.ds(pl.multiple_of(j * 2 * tok, 2 * tok), 2 * tok)
        for e in range(exp_dev):
            gate_pre = mm(x_all[rows, :], wg[e], NN)
            up_pre = mm(x_all[rows, :], wu[e], NN)
            d_mid = mm(g_all[rows, :], wd[pl.ds(e * ff, ff), :], NT)
            weight = wcol[e, rows, 0:1]
            sigma = jax.nn.sigmoid(gate_pre)
            hidden = gate_pre * sigma * up_pre
            dots = jnp.sum(hidden * d_mid, axis=1, keepdims=True)
            dcol[e, rows, :] = jnp.broadcast_to(dots, (2 * tok, 128))
            d_hidden = weight * d_mid
            mid[rows, pl.ds(e * ff, ff)] = (weight * hidden).astype(BF16)
            dgu[rows, pl.ds((exp_dev + e) * ff, ff)] = (d_hidden * gate_pre * sigma).astype(BF16)
            dgu[rows, pl.ds(e * ff, ff)] = (
                d_hidden * up_pre * sigma * (1.0 + gate_pre * (1.0 - sigma))
            ).astype(BF16)

    def stage_two(j):
        rows = pl.ds(pl.multiple_of(j * 2 * tok, 2 * tok), 2 * tok)

        def tile(t, carry):
            cols = pl.ds(pl.multiple_of(t * 512, 512), 512)
            parts_m[rows, cols] = mm(mid[rows, :], wd[:, cols], NN).astype(BF16)
            total = None
            for e in range(exp_dev):
                for w, base in ((wg, 0), (wu, exp_dev)):
                    term = mm(dgu[rows, pl.ds((base + e) * ff, ff)], w[e, cols, :], NT)
                    total = term if total is None else total + term
            parts_r[rows, cols] = total.astype(BF16)
            return carry

        lax.fori_loop(0, model // 512, tile, 0)

    def pair(j, carry):
        stage_one(j)
        for part in range(2):
            @pl.when(j < 3)
            def _():
                for side in range(2):
                    late(side, j, part).wait_recv()

            @pl.when(j < 2)
            def _():
                for side in range(2):
                    late(side, j + 1, part).start()

            if part == 0:
                stage_two(j)

        @pl.when(j == 1)
        def _():
            for side in range(2):
                back_copy(side, 0).start()

        return carry

    lax.fori_loop(0, 4, pair, 0)
    for side in range(2):
        back_copy(side, 1).start()

    stacked = jnp.zeros((tok, 128), F32)
    for slot in range(n):
        for e in range(exp_dev):
            stacked = jnp.where(lane == slot * 8 + e, dcol[e, pl.ds(slot * tok, tok), :], stacked)
    dsend[...] = jnp.transpose(stacked)[: n * 8].reshape(n, 8, 128)

    def dots_copy(slot):
        return pltpu.make_async_remote_copy(
            src_ref=dsend.at[slot], dst_ref=back.at[me],
            send_sem=small_send.at[1, slot], recv_sem=small_recv.at[1, slot],
            device_id={"expert": device_at(pos - step_of(slot))}, device_id_type=MESH,
        )

    for slot in range(1, n):
        dots_copy(slot).start()
    own_dots = pltpu.make_async_copy(dsend.at[0], back.at[me], local_sem.at[0])
    own_dots.start()

    def piece_rows(piece):
        return pl.ds(pl.multiple_of(piece * quarter, quarter), quarter)

    def weight_grads(piece):
        def tile(t, carry):
            base = pl.multiple_of(piece * quarter + t * 256, 256)
            for c in range(2):
                cols = pl.ds(c * exp_dev * ff, exp_dev * ff)
                dwgu[pl.ds(base, 256), cols] = mm(
                    x_all[:, pl.ds(base, 256)], dgu[:, cols], TN
                ).astype(BF16)
            return carry

        lax.fori_loop(0, quarter // 256, tile, 0)

        def tile_down(t, carry):
            at = pl.multiple_of(t * 256, 256)
            dwd[piece, pl.ds(at, 256), :] = mm(
                mid[:, pl.ds(at, 256)], g_all[:, piece_rows(piece)], TN
            ).astype(BF16)
            return carry

        lax.fori_loop(0, exp_dev * ff // 256, tile_down, 0)

    def swap_copies(piece, where):
        return [
            pltpu.make_async_remote_copy(
                src_ref=src, dst_ref=dst, send_sem=dp_send.at[at], recv_sem=dp_recv.at[at],
                device_id={"dp": partner}, device_id_type=MESH,
            )
            for src, dst, at in (
                (dwgu.at[piece_rows(piece)], pr_gu.at[where], 2 * where),
                (dwd.at[piece], pr_d.at[where], 2 * where + 1),
            )
        ]

    far_own, far_partner = (1 - xpos) * 2 + core, (1 - xpos) * 2 + 1 - core
    near_own, near_partner = xpos * 2 + core, xpos * 2 + 1 - core
    far_swap = swap_copies(far_partner, 0)
    near_swap = swap_copies(near_partner, 1)
    far_send = [
        pltpu.make_async_remote_copy(
            src_ref=src, dst_ref=dst, send_sem=dp_send.at[at], recv_sem=dp_recv.at[at],
            device_id={"dp": across}, device_id_type=MESH,
        )
        for src, dst, at in (
            (dwgu.at[piece_rows(far_own)], xr_gu, 4),
            (dwd.at[far_own], xr_d, 5),
        )
    ]

    def return_step(index):
        for side in range(2):
            kind, step = orders[side][index]
            buf, base = bufs[kind], slot_of(step) * tok
            back_copy(side, index - 2).wait_recv()

            def add(t, carry):
                rows = pl.ds(pl.multiple_of(base + t * 32, 32), 32)
                got = landed[side, index - 2, pl.ds(pl.multiple_of(t * 32, 32), 32), :]
                buf[rows, :] = (buf[rows, :].astype(F32) + got.astype(F32)).astype(BF16)
                return carry

            lax.fori_loop(0, tok // 32, add, 0)
            back_copy(side, index).start()

    weight_grads(far_partner)
    for copy in far_swap:
        copy.start()
    return_step(2)
    weight_grads(far_own)
    for copy in far_swap:
        copy.wait_recv()

    def add_far(t, carry):
        rows = pl.ds(pl.multiple_of(far_own * quarter + t * 32, 32), 32)
        got = pr_gu[0, pl.ds(pl.multiple_of(t * 32, 32), 32), :]
        dwgu[rows, :] = (dwgu[rows, :].astype(F32) + got.astype(F32)).astype(BF16)
        return carry

    lax.fori_loop(0, quarter // 32, add_far, 0)
    far_send[0].start()

    def add_far_down(t, carry):
        rows = pl.ds(pl.multiple_of(t * 32, 32), 32)
        dwd[far_own, rows, :] = (
            dwd[far_own, rows, :].astype(F32) + pr_d[0, rows, :].astype(F32)
        ).astype(BF16)
        return carry

    lax.fori_loop(0, exp_dev * ff // 32, add_far_down, 0)
    far_send[1].start()
    return_step(3)
    weight_grads(near_partner)
    for copy in near_swap:
        copy.start()
    return_step(4)
    weight_grads(near_own)
    return_step(5)

    own_dots.wait()
    for slot in range(1, n):
        dots_copy(slot).wait_recv()
    got = jnp.concatenate(
        [back[...].reshape(n * 8, 128), jnp.zeros((128 - n * 8, 128), F32)], axis=0
    )
    got = jnp.transpose(got)
    result = jnp.zeros((tok, 128), F32)
    for k in range(ids_ref.shape[1]):
        mine = jnp.sum(
            jnp.where(ids_ref[:, k : k + 1] == expert_of_lane, got, 0.0), axis=1, keepdims=True
        )
        result = jnp.where(lane == k, mine, result)
    dgates_ref[...] = result[:, : ids_ref.shape[1]]
    return_step(6)

    for copy in near_swap:
        copy.wait_recv()
    for copy in far_send:
        copy.wait_recv()

    def final_gu(t, carry):
        rows = pl.ds(pl.multiple_of(t * 32, 32), 32)
        own = pl.ds(pl.multiple_of(near_own * quarter + t * 32, 32), 32)
        total = (
            dwgu[own, :].astype(F32) + pr_gu[1, rows, :].astype(F32) + xr_gu[rows, :].astype(F32)
        ).astype(BF16)
        for e in range(exp_dev):
            ogate_ref[e, rows, :] = total[:, e * ff : (e + 1) * ff]
            oup_ref[e, rows, :] = total[:, (exp_dev + e) * ff : (exp_dev + e + 1) * ff]
        return carry

    lax.fori_loop(0, quarter // 32, final_gu, 0)
    for e in range(exp_dev):
        def final_down(t, carry):
            at = pl.multiple_of(t * 32, 32)
            rows = pl.ds(pl.multiple_of(e * ff + at, 32), 32)
            odown_ref[e, pl.ds(at, 32), :] = (
                dwd[near_own, rows, :].astype(F32)
                + pr_d[1, rows, :].astype(F32)
                + xr_d[rows, :].astype(F32)
            ).astype(BF16)
            return carry

        lax.fori_loop(0, ff // 32, final_down, 0)

    for index in (5, 6):
        for side in range(2):
            back_copy(side, index).wait_recv()
        kind = orders[0][index][0]
        other = orders[1][index][0]
        for side, name in ((0, kind), (1, other)):
            buf, out = bufs[name], {"m": mixed_ref, "r": dtok_ref}[name]

            def close(t, carry):
                rows = pl.ds(pl.multiple_of(t * 32, 32), 32)
                so_far = buf if index == 5 else out
                out[rows, :] = (
                    so_far[rows, :].astype(F32) + landed[side, index, rows, :].astype(F32)
                ).astype(BF16)
                return carry

            lax.fori_loop(0, tok // 32, close, 0)

    for side in range(2):
        for index in range(8):
            early(side, index).wait_send()
        for hop in range(3):
            for part in range(2):
                late(side, hop, part).wait_send()
        for index in range(7):
            back_copy(side, index).wait_send()
    for k in range(1, n):
        gate_copy(k).wait_send()
        dots_copy(k).wait_send()
    for copy in far_swap + near_swap + far_send:
        copy.wait_send()


def local(tokens, expert_ids, gate_weights, grad_out, w_gate, w_up, w_down):
    owners, dps = lax.axis_size("expert"), lax.axis_size("dp")
    if owners != 8 or dps != 4:
        return local_wide(tokens, expert_ids, gate_weights, grad_out, w_gate, w_up, w_down)
    tok, model = tokens.shape
    exp_dev, _, ff = w_gate.shape
    rows, mids = owners * tok, exp_dev * ff
    quarter = model // dps
    hbm = pl.BlockSpec(memory_space=pl.ANY)
    vmem = pl.BlockSpec(memory_space=pltpu.VMEM)
    dma = pltpu.SemaphoreType.DMA
    out = pl.pallas_call(
        layer_kernel,
        out_shape=(
            jax.ShapeDtypeStruct((tok, model), BF16),
            jax.ShapeDtypeStruct((tok, model), BF16),
            jax.ShapeDtypeStruct(gate_weights.shape, F32),
            jax.ShapeDtypeStruct((exp_dev, quarter, ff), BF16),
            jax.ShapeDtypeStruct((exp_dev, quarter, ff), BF16),
            jax.ShapeDtypeStruct((exp_dev, ff, quarter), BF16),
        ),
        in_specs=[hbm] * 5 + [vmem] * 2,
        out_specs=[vmem] * 6,
        scratch_shapes=[
            pltpu.VMEM((rows, model), BF16),
            pltpu.VMEM((rows, model), BF16),
            pltpu.VMEM((exp_dev, model, ff), BF16),
            pltpu.VMEM((exp_dev, model, ff), BF16),
            pltpu.VMEM((mids, model), BF16),
            pltpu.VMEM((rows, model), BF16),
            pltpu.VMEM((rows, model), BF16),
            pltpu.VMEM((rows, 2 * mids), BF16),
            pltpu.VMEM((rows, mids), BF16),
            pltpu.VMEM((model, 2 * mids), BF16),
            pltpu.VMEM((dps, mids, quarter), BF16),
            pltpu.VMEM((2, 7, tok, model), BF16),
            pltpu.VMEM((2, quarter, 2 * mids), BF16),
            pltpu.VMEM((2, mids, quarter), BF16),
            pltpu.VMEM((quarter, 2 * mids), BF16),
            pltpu.VMEM((mids, quarter), BF16),
            pltpu.VMEM((owners, 8, 128), F32),
            pltpu.VMEM((owners, 8, 128), F32),
            pltpu.VMEM((exp_dev, rows, 128), F32),
            pltpu.VMEM((exp_dev, rows, 128), F32),
            pltpu.VMEM((owners, 8, 128), F32),
            pltpu.VMEM((owners, 8, 128), F32),
            dma((5,)),
            dma((2, 14)),
            dma((2, 14)),
            dma((2, 7)),
            dma((2, 7)),
            dma((2, 8)),
            dma((2, 8)),
            dma((6,)),
            dma((6,)),
        ],
        compiler_params=pltpu.CompilerParams(
            collective_id=0, has_side_effects=True, vmem_limit_bytes=67_043_328
        ),
        name="moe_layer",
    )(tokens, grad_out, w_gate, w_up, w_down.reshape(mids, model), expert_ids, gate_weights)
    return tuple(out)


def solution(mesh):
    in_specs = (
        P(("dp", "expert"), None),
        P(("dp", "expert"), None),
        P(("dp", "expert"), None),
        P(("dp", "expert"), None),
        P("expert", None, None),
        P("expert", None, None),
        P("expert", None, None),
    )
    out_specs = (
        P(("dp", "expert"), None),
        P(("dp", "expert"), None),
        P(("dp", "expert"), None),
        P("expert", "dp", None),
        P("expert", "dp", None),
        P("expert", None, "dp"),
    )
    return jax.shard_map(local, mesh=mesh, in_specs=in_specs, out_specs=out_specs, check_vma=False)
```

profile of v0, /device:TPU:0, one launch (start us, length us, event | category | flops | bytes accessed | tf_op | source)
XLA Modules:
  0.0 182.5 jit_solution(17311494736949176111)
XLA Ops:
  0.6 1.4 copy.13.ids_ref
  2.0 1.4 copy.14.gw_ref
  3.5 169.8 %moe_layer.1 = (bf16[128,2048]{1,0:T(8,128)(2,1)}, bf16[128,2048]{1,0:T(8,128)(2,1)}, f32[128,4]{1,0:T(8,128)}, bf16[2,512,384]{2,1,0:T(8,128)(2,1)}, bf16[2,512...) custom-call(bf16[128,2048]{1,0:T(8,128)(2,1)} %tok_in.1, bf16[128,2048]{1,0:T(8,128)(2,1)} %grad_in.1, ...), custom_call_target="tpu_custom_call" | custom-call | tf_op jit(solution)/shard_map/moe_layer/pallas_call | solution.py:494
  173.2 0.0 copy-start.1
  173.3 0.0 copy-start
  173.3 1.6 copy.15
  174.9 1.9 %copy.21 = bf16[128,2048]{1,0:T(8,128)(2,1)} copy(bf16[128,2048]{1,0:T(8,128)(2,1)} %get-tuple-element.18) | data formatting | bytes 1048576
  176.8 1.9 %copy.22 = bf16[128,2048]{1,0:T(8,128)(2,1)} copy(bf16[128,2048]{1,0:T(8,128)(2,1)} %get-tuple-element.19) | data formatting | bytes 1048576
  178.6 2.1 %copy.23 = bf16[2,512,384]{2,1,0:T(8,128)(2,1)} copy(bf16[2,512,384]{2,1,0:T(8,128)(2,1)} %get-tuple-element.21) | data formatting | bytes 1572864
  180.7 0.0 copy-done.1
  180.7 0.9 copy.24
  181.6 0.0 copy-done
  181.6 0.9 copy.25
Async XLA Ops:
  173.2 7.5 %copy-start.1 = (bf16[2,512,384]{2,1,0:T(8,128)(2,1)S(1)}, bf16[2,512,384]{2,1,0:T(8,128)(2,1)}, u32[]{:S(2)}) copy-start(bf16[2,512,384]{2,1,0:T(8,128)(2,1)} %get-tuple-element.22) | copy-start | bytes 2359300
  173.3 8.4 %copy-start = (bf16[2,384,512]{2,1,0:T(8,128)(2,1)S(1)}, bf16[2,384,512]{2,1,0:T(8,128)(2,1)}, u32[]{:S(2)}) copy-start(bf16[2,384,512]{2,1,0:T(8,128)(2,1)} %get-tuple-element.23) | copy-start | bytes 2359300
where the time goes:
time: 183 us; the launch traced here: 182 us
  Pallas kernels  170 us (93%)
  local copies, waits for them, and re-layouts  12.1 us (7%)
    pallas_call x1, Pallas kernels, local(): pl.pallas_call(layer_kernel, out_shape=(jax.ShapeDtypeStruct((tok, model)...  170 us
    unnamed x11, local copies, waits for them, and re-layouts  10.4 us

commit v1 on v0

--- a/solution.py
+++ b/solution.py
@@ -165,12 +165,13 @@
         for side in range(2):
             early(side, part).start()
 
-    lane = lax.broadcasted_iota(jnp.int32, (tok, 128), 1)
-    expert_of_lane = jnp.where(lane % 8 < exp_dev, (lane // 8) * exp_dev + lane % 8, -1)
-    gates = jnp.zeros((tok, 128), F32)
-    for k in range(ids_ref.shape[1]):
-        gates = gates + jnp.where(ids_ref[:, k : k + 1] == expert_of_lane, gw_ref[:, k : k + 1], 0.0)
-    gsend[...] = jnp.transpose(gates)[: n * 8].reshape(n, 8, 128)
+    line = lax.broadcasted_iota(jnp.int32, (n * 8, tok), 0)
+    expert_of_line = jnp.where(line % 8 < exp_dev, (line // 8) * exp_dev + line % 8, -1)
+    top = ids_ref.shape[0]
+    gates = jnp.zeros((n * 8, tok), F32)
+    for k in range(top):
+        gates = gates + jnp.where(ids_ref[k : k + 1, :] == expert_of_line, gw_ref[k : k + 1, :], 0.0)
+    gsend[...] = gates.reshape(n, 8, tok)
 
     def gate_copy(k):
         slot = slot_of(k if k <= 4 else k - 8)
@@ -283,6 +284,7 @@
     for side in range(2):
         back_copy(side, 1).start()
 
+    lane = lax.broadcasted_iota(jnp.int32, (tok, 128), 1)
     stacked = jnp.zeros((tok, 128), F32)
     for slot in range(n):
         for e in range(exp_dev):
@@ -404,17 +406,11 @@
     own_dots.wait()
     for slot in range(1, n):
         dots_copy(slot).wait_recv()
-    got = jnp.concatenate(
-        [back[...].reshape(n * 8, 128), jnp.zeros((128 - n * 8, 128), F32)], axis=0
-    )
-    got = jnp.transpose(got)
-    result = jnp.zeros((tok, 128), F32)
-    for k in range(ids_ref.shape[1]):
-        mine = jnp.sum(
-            jnp.where(ids_ref[:, k : k + 1] == expert_of_lane, got, 0.0), axis=1, keepdims=True
-        )
-        result = jnp.where(lane == k, mine, result)
-    dgates_ref[...] = result[:, : ids_ref.shape[1]]
+    got = back[...].reshape(n * 8, tok)
+    for k in range(top):
+        dgates_ref[k : k + 1, :] = jnp.sum(
+            jnp.where(ids_ref[k : k + 1, :] == expert_of_line, got, 0.0), axis=0, keepdims=True
+        )
     return_step(6)
 
     for copy in near_swap:
@@ -478,6 +474,19 @@
         dots_copy(k).wait_send()
     for copy in far_swap + near_swap + far_send:
         copy.wait_send()
+
+
+def hand_over(*refs):
+    held, sem = refs[12:18], refs[18]
+    inward = [pltpu.make_async_copy(refs[i], held[i], sem.at[0, i]) for i in range(6)]
+    outward = [pltpu.make_async_copy(held[i], refs[6 + i], sem.at[1, i]) for i in range(6)]
+    for copy in inward:
+        copy.start()
+    for i in range(6):
+        inward[i].wait()
+        outward[i].start()
+    for copy in outward:
+        copy.wait()
 
 
 def local(tokens, expert_ids, gate_weights, grad_out, w_gate, w_up, w_down):
@@ -496,7 +505,7 @@
         out_shape=(
             jax.ShapeDtypeStruct((tok, model), BF16),
             jax.ShapeDtypeStruct((tok, model), BF16),
-            jax.ShapeDtypeStruct(gate_weights.shape, F32),
+            jax.ShapeDtypeStruct(gate_weights.shape[::-1], F32),
             jax.ShapeDtypeStruct((exp_dev, quarter, ff), BF16),
             jax.ShapeDtypeStruct((exp_dev, quarter, ff), BF16),
             jax.ShapeDtypeStruct((exp_dev, ff, quarter), BF16),
@@ -540,8 +549,17 @@
             collective_id=0, has_side_effects=True, vmem_limit_bytes=67_043_328
         ),
         name="moe_layer",
-    )(tokens, grad_out, w_gate, w_up, w_down.reshape(mids, model), expert_ids, gate_weights)
-    return tuple(out)
+    )(tokens, grad_out, w_gate, w_up, w_down.reshape(mids, model), expert_ids.T, gate_weights.T)
+    out = pl.pallas_call(
+        hand_over,
+        out_shape=tuple(jax.ShapeDtypeStruct(v.shape, v.dtype) for v in out),
+        in_specs=[hbm] * 6,
+        out_specs=[hbm] * 6,
+        scratch_shapes=[pltpu.VMEM(v.shape, v.dtype) for v in out] + [dma((2, 6))],
+        compiler_params=pltpu.CompilerParams(vmem_limit_bytes=67_043_328),
+        name="hand_over",
+    )(*out)
+    return (out[0], out[1], out[2].T, *out[3:])
 
 
 def solution(mesh):

time: 183 us -> 173 us (0.945)
  local copies, waits for them, and re-layouts: 12.1 us -> 0 us
  Pallas kernels: 170 us -> 173 us
    unnamed x11 -> x0, local copies, waits for them, and re-layouts: 10.4 us -> none
    pallas_call x0 -> x1, Pallas kernels: none -> 2.96 us  [local(): pl.pallas_call(hand_over, out_shape=tuple((jax.ShapeDtypeStruct(v.shape,...]
where the time goes in v1:
time: 173 us
  Pallas kernels  173 us (100%)
    pallas_call x1, Pallas kernels, local(): pl.pallas_call(layer_kernel, out_shape=(jax.ShapeDtypeStruct((tok, model)...  170 us

profile of v1, /device:TPU:0, one launch (start us, length us, event | category | flops | bytes accessed | tf_op | source)
XLA Modules:
  0.0 173.2 jit_solution(4098610722937058325)
XLA Ops:
  0.6 169.6 %moe_layer.1 = (bf16[128,2048]{1,0:T(8,128)(2,1)}, bf16[128,2048]{1,0:T(8,128)(2,1)}, f32[4,128]{1,0:T(4,128)}, bf16[2,512,384]{2,1,0:T(8,128)(2,1)}, bf16[2,512...) custom-call(bf16[128,2048]{1,0:T(8,128)(2,1)} %tok_in.1, bf16[128,2048]{1,0:T(8,128)(2,1)} %grad_in.1, ...), custom_call_target="tpu_custom_call" | custom-call | tf_op jit(solution)/shard_map/moe_layer/pallas_call | solution.py:503
  170.2 3.0 %hand_over.1 = (bf16[128,2048]{1,0:T(8,128)(2,1)}, bf16[128,2048]{1,0:T(8,128)(2,1)}, f32[4,128]{1,0:T(4,128)}, bf16[2,512,384]{2,1,0:T(8,128)(2,1)}, bf16[2,512...) custom-call(bf16[128,2048]{1,0:T(8,128)(2,1)} %get-tuple-element.18.refs_0_, ...), custom_call_target="tpu_custom_call" | custom-call | tf_op jit(solution)/shard_map/hand_over/pallas_call | solution.py:553

commit v2 on v1

--- a/solution.py
+++ b/solution.py
@@ -64,6 +64,9 @@
     return (mixed_out, d_tokens, d_gates, grad_gate, grad_up, grad_down)
 
 
+CAP_DEV = 48
+
+
 def slot_of(step):
     if step == 0:
         return 0
@@ -89,12 +92,14 @@
     mixed_ref, dtok_ref, dgates_ref, ogate_ref, oup_ref, odown_ref,
     x_all, g_all, wg, wu, wd, parts_m, parts_r, dgu, mid, dwgu, dwd, landed,
     pr_gu, pr_d, xr_gu, xr_d, gsend, grecv, wcol, dcol, dsend, back,
+    pick, packed,
     local_sem, ag_send, ag_recv, rs_send, rs_recv, small_send, small_recv, dp_send, dp_recv,
 ):
     n = 8
     tok, model = tok_in.shape
     exp_dev, ff = wg.shape[0], wg.shape[2]
     half = tok // 2
+    few = pick.shape[1]
     quarter = model // 4
     me = lax.axis_index("expert")
     dp = lax.axis_index("dp")
@@ -161,6 +166,49 @@
             side, 8 + 2 * hop + part,
         )
 
+    def packed_copy(side, last):
+        landing = (parts_m, parts_r)[side]
+        return send_to(
+            packed.at[side, last], landing.at[pl.ds((6 + last) * tok, few)], side, 6 + 6 * last
+        )
+
+    def squeeze(which, src, base, dst):
+        def tile(t, carry):
+            cols = pl.ds(pl.multiple_of(t * 512, 512), 512)
+            dst[pl.ds(0, few), cols] = mm(
+                pick[which], src[pl.ds(base, tok), cols], NN
+            ).astype(BF16)
+            return carry
+
+        lax.fori_loop(0, model // 512, tile, 0)
+
+    def spread(which, src, base, dst, at):
+        def tile(t, carry):
+            cols = pl.ds(pl.multiple_of(t * 512, 512), 512)
+            dst[pl.ds(at, tok), cols] = mm(
+                pick[which], src[pl.ds(base, few), cols], TN
+            ).astype(BF16)
+            return carry
+
+        lax.fori_loop(0, model // 512, tile, 0)
+
+    def send_packed(side, last):
+        if side == 0:
+            src, slot, which = ((x_all, 6, 3), (g_all, 4, 4))[last]
+        else:
+            src, slot, which = ((g_all, 7, 5), (x_all, 5, 6))[last]
+        squeeze(which, src, slot * tok, packed.at[side, last])
+        packed_copy(side, last).start()
+
+    def take_packed(side, last):
+        packed_copy(side, last).wait_recv()
+        landing = (parts_m, parts_r)[side]
+        if side == 0:
+            dst, slot, which = ((x_all, 1, 0), (g_all, 6, 1))[last]
+        else:
+            dst, slot, which = ((g_all, 1, 0), (x_all, 7, 2))[last]
+        spread(which, landing, (6 + last) * tok, dst, slot * tok)
+
     for part in range(2):
         for side in range(2):
             early(side, part).start()
@@ -182,24 +230,41 @@
             device_id={"expert": to}, device_id_type=MESH,
         )
 
+    RELAYS = ((3, 4), (2, 3), (-3, -4), (-2, -3))
+
+    def relay_gates(case):
+        to, owner = (device_at(pos + k) for k in RELAYS[case])
+        return pltpu.make_async_remote_copy(
+            src_ref=gsend.at[owner], dst_ref=grecv.at[n + case],
+            send_sem=small_send.at[0, n + case], recv_sem=small_recv.at[0, n + case],
+            device_id={"expert": to}, device_id_type=MESH,
+        )
+
     for k in range(1, n):
         gate_copy(k).start()
+    for case in range(4):
+        relay_gates(case).start()
     grecv[0] = gsend[me]
     locals_[0].wait()
     locals_[1].wait()
 
-    for index in range(8):
+    for index in range(6):
         for side in range(2):
             early(side, index).wait_recv()
-            if index < 6:
+            if index < 4:
                 early(side, index + 2).start()
+            elif index == 4:
+                late(side, 0, 0).start()
             else:
-                late(side, 0, index - 6).start()
+                send_packed(side, 0)
+                late(side, 0, 1).start()
         if index == 1:
             for k in range(1, n):
                 gate_copy(k).wait_recv()
+            for case in range(4):
+                relay_gates(case).wait_recv()
             cols = jnp.concatenate(
-                [grecv[...].reshape(n * 8, 128), jnp.zeros((128 - n * 8, 128), F32)], axis=0
+                [grecv[pl.ds(0, n)].reshape(n * 8, 128), jnp.zeros((128 - n * 8, 128), F32)], axis=0
             )
             cols = jnp.transpose(cols)
             for slot in range(n):
@@ -208,20 +273,46 @@
                     wcol[e, pl.ds(slot * tok, tok), :] = jnp.broadcast_to(
                         cols[:, at : at + 1], (tok, 128)
                     )
+            earlier = (
+                lax.broadcasted_iota(jnp.int32, (tok, tok), 0)
+                < lax.broadcasted_iota(jnp.int32, (tok, tok), 1)
+            ).astype(F32).astype(BF16)
+            place = lax.broadcasted_iota(jnp.int32, (few, tok), 0).astype(F32)
+            for which, slot in enumerate((1, 6, 7, 8, 9, 10, 11)):
+                needed = jnp.max(grecv[slot], axis=0, keepdims=True) > 0.0
+                needed = jnp.broadcast_to(jnp.where(needed, 1.0, 0.0), (8, tok))
+                rank = mm(needed.astype(BF16), earlier, NN)
+                rank = jnp.where(needed > 0.0, rank, -1.0)[0:1, :]
+                pick[which] = jnp.where(place == rank, 1.0, 0.0).astype(BF16)
         if index == 3:
             for copy in locals_[2:]:
                 copy.wait()
+    for side in range(2):
+        late(side, 0, 0).wait_recv()
+        late(side, 1, 0).start()
+    for side in range(2):
+        take_packed(side, 0)
 
     bufs = {"m": parts_m, "r": parts_r}
     orders = (RETURN_RIGHT, RETURN_LEFT)
 
     def back_copy(side, index):
         kind, step = orders[side][index]
+        rows = few if index < 2 else tok
         return pltpu.make_async_remote_copy(
-            src_ref=bufs[kind].at[pl.ds(slot_of(step) * tok, tok)], dst_ref=landed.at[side, index],
+            src_ref=bufs[kind].at[pl.ds(slot_of(step) * tok, rows)],
+            dst_ref=landed.at[side, index, pl.ds(0, rows)],
             send_sem=rs_send.at[side, index], recv_sem=rs_recv.at[side, index],
             device_id={"expert": sides[side]}, device_id_type=MESH,
         )
+
+    def return_first(index):
+        for side in range(2):
+            kind, step = orders[side][index]
+            base = slot_of(step) * tok
+            which = 0 if index == 0 else 2 - side
+            squeeze(which, bufs[kind], base, bufs[kind].at[pl.ds(base, tok)])
+            back_copy(side, index).start()
 
     def stage_one(j):
         rows = pl.ds(pl.multiple_of(j * 2 * tok, 2 * tok), 2 * tok)
@@ -258,31 +349,33 @@
         lax.fori_loop(0, model // 512, tile, 0)
 
     def pair(j, carry):
+        @pl.when(j == 3)
+        def _():
+            for side in range(2):
+                take_packed(side, 1)
+
         stage_one(j)
-        for part in range(2):
-            @pl.when(j < 3)
-            def _():
-                for side in range(2):
-                    late(side, j, part).wait_recv()
-
-            @pl.when(j < 2)
-            def _():
-                for side in range(2):
-                    late(side, j + 1, part).start()
-
-            if part == 0:
-                stage_two(j)
+
+        @pl.when(j == 0)
+        def _():
+            for side in range(2):
+                late(side, 0, 1).wait_recv()
+                late(side, 1, 1).start()
 
         @pl.when(j == 1)
         def _():
+            for part in range(2):
+                for side in range(2):
+                    late(side, 1, part).wait_recv()
             for side in range(2):
-                back_copy(side, 0).start()
-
+                send_packed(side, 1)
+            return_first(0)
+
+        stage_two(j)
         return carry
 
     lax.fori_loop(0, 4, pair, 0)
-    for side in range(2):
-        back_copy(side, 1).start()
+    return_first(1)
 
     lane = lax.broadcasted_iota(jnp.int32, (tok, 128), 1)
     stacked = jnp.zeros((tok, 128), F32)
@@ -359,6 +452,18 @@
             kind, step = orders[side][index]
             buf, base = bufs[kind], slot_of(step) * tok
             back_copy(side, index - 2).wait_recv()
+            if index < 4:
+                which = (5, 3)[side] if index == 2 else (6, 4)[side]
+
+                def unpack(t, carry):
+                    rows, cols = pl.ds(base, tok), pl.ds(pl.multiple_of(t * 512, 512), 512)
+                    got = mm(pick[which], landed[side, index - 2, pl.ds(0, few), cols], TN)
+                    buf[rows, cols] = (buf[rows, cols].astype(F32) + got).astype(BF16)
+                    return carry
+
+                lax.fori_loop(0, model // 512, unpack, 0)
+                back_copy(side, index).start()
+                continue
 
             def add(t, carry):
                 rows = pl.ds(pl.multiple_of(base + t * 32, 32), 32)
@@ -462,9 +567,11 @@
             lax.fori_loop(0, tok // 32, close, 0)
 
     for side in range(2):
-        for index in range(8):
+        for index in range(6):
             early(side, index).wait_send()
-        for hop in range(3):
+        for last in range(2):
+            packed_copy(side, last).wait_send()
+        for hop in range(2):
             for part in range(2):
                 late(side, hop, part).wait_send()
         for index in range(7):
@@ -472,6 +579,8 @@
     for k in range(1, n):
         gate_copy(k).wait_send()
         dots_copy(k).wait_send()
+    for case in range(4):
+        relay_gates(case).wait_send()
     for copy in far_swap + near_swap + far_send:
         copy.wait_send()
 
@@ -491,12 +600,13 @@
 
 def local(tokens, expert_ids, gate_weights, grad_out, w_gate, w_up, w_down):
     owners, dps = lax.axis_size("expert"), lax.axis_size("dp")
-    if owners != 8 or dps != 4:
+    if (owners, dps, *w_gate.shape[:1], tokens.shape[0]) != (8, 4, 2, 128):
         return local_wide(tokens, expert_ids, gate_weights, grad_out, w_gate, w_up, w_down)
     tok, model = tokens.shape
     exp_dev, _, ff = w_gate.shape
     rows, mids = owners * tok, exp_dev * ff
     quarter = model // dps
+    few = exp_dev * CAP_DEV
     hbm = pl.BlockSpec(memory_space=pl.ANY)
     vmem = pl.BlockSpec(memory_space=pltpu.VMEM)
     dma = pltpu.SemaphoreType.DMA
@@ -530,18 +640,20 @@
             pltpu.VMEM((quarter, 2 * mids), BF16),
             pltpu.VMEM((mids, quarter), BF16),
             pltpu.VMEM((owners, 8, 128), F32),
-            pltpu.VMEM((owners, 8, 128), F32),
+            pltpu.VMEM((owners + 4, 8, 128), F32),
             pltpu.VMEM((exp_dev, rows, 128), F32),
             pltpu.VMEM((exp_dev, rows, 128), F32),
             pltpu.VMEM((owners, 8, 128), F32),
             pltpu.VMEM((owners, 8, 128), F32),
+            pltpu.VMEM((7, few, tok), BF16),
+            pltpu.VMEM((2, 2, few, model), BF16),
             dma((5,)),
             dma((2, 14)),
             dma((2, 14)),
             dma((2, 7)),
             dma((2, 7)),
-            dma((2, 8)),
-            dma((2, 8)),
+            dma((2, 12)),
+            dma((2, 12)),
             dma((6,)),
             dma((6,)),
         ],

time: 173 us -> 171 us (0.988)
  Pallas kernels: 173 us -> 171 us
    pallas_call x1, Pallas kernels: 170 us -> 168 us  [local(): pl.pallas_call(layer_kernel, out_shape=(jax.ShapeDtypeStruct((tok, model)...]
where the time goes in v2:
time: 171 us
  Pallas kernels  171 us (100%)
    pallas_call x1, Pallas kernels, local(): pl.pallas_call(layer_kernel, out_shape=(jax.ShapeDtypeStruct((tok, model)...  168 us

profile of v2, /device:TPU:0, one launch (start us, length us, event | category | flops | bytes accessed | tf_op | source)
XLA Modules:
  0.0 171.2 jit_solution(5707020935680312779)
XLA Ops:
  0.6 167.6 %moe_layer.1 = (bf16[128,2048]{1,0:T(8,128)(2,1)}, bf16[128,2048]{1,0:T(8,128)(2,1)}, f32[4,128]{1,0:T(4,128)}, bf16[2,512,384]{2,1,0:T(8,128)(2,1)}, bf16[2,512...) custom-call(bf16[128,2048]{1,0:T(8,128)(2,1)} %tok_in.1, bf16[128,2048]{1,0:T(8,128)(2,1)} %grad_in.1, ...), custom_call_target="tpu_custom_call" | custom-call | tf_op jit(solution)/shard_map/moe_layer/pallas_call | solution.py:613
  168.3 3.0 %hand_over.1 = (bf16[128,2048]{1,0:T(8,128)(2,1)}, bf16[128,2048]{1,0:T(8,128)(2,1)}, f32[4,128]{1,0:T(4,128)}, bf16[2,512,384]{2,1,0:T(8,128)(2,1)}, bf16[2,512...) custom-call(bf16[128,2048]{1,0:T(8,128)(2,1)} %get-tuple-element.18.refs_0_, ...), custom_call_target="tpu_custom_call" | custom-call | tf_op jit(solution)/shard_map/hand_over/pallas_call | solution.py:665

commit v3 on v2

--- a/solution.py
+++ b/solution.py
@@ -90,9 +90,9 @@
 def layer_kernel(
     tok_in, grad_in, wg_in, wu_in, wd_in, ids_ref, gw_ref,
     mixed_ref, dtok_ref, dgates_ref, ogate_ref, oup_ref, odown_ref,
-    x_all, g_all, wg, wu, wd, parts_m, parts_r, dgu, mid, dwgu, dwd, landed,
+    x_all, g_all, wg, wu, wd, parts_m, parts_r, dgu, mid, dwgu, dwd, landed, landed_few,
     pr_gu, pr_d, xr_gu, xr_d, gsend, grecv, wcol, dcol, dsend, back,
-    pick, packed,
+    pick, packed, sgate, sup, sdown,
     local_sem, ag_send, ag_recv, rs_send, rs_recv, small_send, small_recv, dp_send, dp_recv,
 ):
     n = 8
@@ -192,13 +192,12 @@
 
         lax.fori_loop(0, model // 512, tile, 0)
 
-    def send_packed(side, last):
+    def pack_last(side, last):
         if side == 0:
             src, slot, which = ((x_all, 6, 3), (g_all, 4, 4))[last]
         else:
             src, slot, which = ((g_all, 7, 5), (x_all, 5, 6))[last]
         squeeze(which, src, slot * tok, packed.at[side, last])
-        packed_copy(side, last).start()
 
     def take_packed(side, last):
         packed_copy(side, last).wait_recv()
@@ -248,16 +247,47 @@
     locals_[0].wait()
     locals_[1].wait()
 
+    def stage_one(base, size):
+        rows = pl.ds(base, size)
+        for e in range(exp_dev):
+            gate_pre = mm(x_all[rows, :], wg[e], NN)
+            up_pre = mm(x_all[rows, :], wu[e], NN)
+            d_mid = mm(g_all[rows, :], wd[pl.ds(e * ff, ff), :], NT)
+            weight = wcol[e, rows, 0:1]
+            sigma = jax.nn.sigmoid(gate_pre)
+            hidden = gate_pre * sigma * up_pre
+            dots = jnp.sum(hidden * d_mid, axis=1, keepdims=True)
+            dcol[e, rows, :] = jnp.broadcast_to(dots, (size, 128))
+            d_hidden = weight * d_mid
+            mid[rows, pl.ds(e * ff, ff)] = (weight * hidden).astype(BF16)
+            dgu[rows, pl.ds((exp_dev + e) * ff, ff)] = (d_hidden * gate_pre * sigma).astype(BF16)
+            dgu[rows, pl.ds(e * ff, ff)] = (
+                d_hidden * up_pre * sigma * (1.0 + gate_pre * (1.0 - sigma))
+            ).astype(BF16)
+
+    def stage_two(mixed_base, rows_base, size):
+        mixed_rows, grad_rows = pl.ds(mixed_base, size), pl.ds(rows_base, size)
+
+        def tile(t, carry):
+            cols = pl.ds(pl.multiple_of(t * 512, 512), 512)
+            parts_m[mixed_rows, cols] = mm(mid[mixed_rows, :], wd[:, cols], NN).astype(BF16)
+            total = None
+            for e in range(exp_dev):
+                for w, base in ((wg, 0), (wu, exp_dev)):
+                    term = mm(dgu[grad_rows, pl.ds((base + e) * ff, ff)], w[e, cols, :], NT)
+                    total = term if total is None else total + term
+            parts_r[grad_rows, cols] = total.astype(BF16)
+            return carry
+
+        lax.fori_loop(0, model // 512, tile, 0)
+
     for index in range(6):
         for side in range(2):
             early(side, index).wait_recv()
             if index < 4:
                 early(side, index + 2).start()
-            elif index == 4:
-                late(side, 0, 0).start()
             else:
-                send_packed(side, 0)
-                late(side, 0, 1).start()
+                late(side, 0, index - 4).start()
         if index == 1:
             for k in range(1, n):
                 gate_copy(k).wait_recv()
@@ -284,14 +314,20 @@
                 rank = mm(needed.astype(BF16), earlier, NN)
                 rank = jnp.where(needed > 0.0, rank, -1.0)[0:1, :]
                 pick[which] = jnp.where(place == rank, 1.0, 0.0).astype(BF16)
-        if index == 3:
+        if index == 2:
             for copy in locals_[2:]:
                 copy.wait()
+            stage_one(0, tok)
+        if index == 3:
+            stage_two(0, 0, tok)
     for side in range(2):
-        late(side, 0, 0).wait_recv()
-        late(side, 1, 0).start()
+        pack_last(side, 0)
+    for part in range(2):
+        for side in range(2):
+            late(side, 0, part).wait_recv()
+            late(side, 1, part).start()
     for side in range(2):
-        take_packed(side, 0)
+        packed_copy(side, 0).start()
 
     bufs = {"m": parts_m, "r": parts_r}
     orders = (RETURN_RIGHT, RETURN_LEFT)
@@ -301,7 +337,7 @@
         rows = few if index < 2 else tok
         return pltpu.make_async_remote_copy(
             src_ref=bufs[kind].at[pl.ds(slot_of(step) * tok, rows)],
-            dst_ref=landed.at[side, index, pl.ds(0, rows)],
+            dst_ref=landed_few.at[side, index] if index < 2 else landed.at[side, index - 2],
             send_sem=rs_send.at[side, index], recv_sem=rs_recv.at[side, index],
             device_id={"expert": sides[side]}, device_id_type=MESH,
         )
@@ -314,68 +350,40 @@
             squeeze(which, bufs[kind], base, bufs[kind].at[pl.ds(base, tok)])
             back_copy(side, index).start()
 
-    def stage_one(j):
-        rows = pl.ds(pl.multiple_of(j * 2 * tok, 2 * tok), 2 * tok)
-        for e in range(exp_dev):
-            gate_pre = mm(x_all[rows, :], wg[e], NN)
-            up_pre = mm(x_all[rows, :], wu[e], NN)
-            d_mid = mm(g_all[rows, :], wd[pl.ds(e * ff, ff), :], NT)
-            weight = wcol[e, rows, 0:1]
-            sigma = jax.nn.sigmoid(gate_pre)
-            hidden = gate_pre * sigma * up_pre
-            dots = jnp.sum(hidden * d_mid, axis=1, keepdims=True)
-            dcol[e, rows, :] = jnp.broadcast_to(dots, (2 * tok, 128))
-            d_hidden = weight * d_mid
-            mid[rows, pl.ds(e * ff, ff)] = (weight * hidden).astype(BF16)
-            dgu[rows, pl.ds((exp_dev + e) * ff, ff)] = (d_hidden * gate_pre * sigma).astype(BF16)
-            dgu[rows, pl.ds(e * ff, ff)] = (
-                d_hidden * up_pre * sigma * (1.0 + gate_pre * (1.0 - sigma))
-            ).astype(BF16)
-
-    def stage_two(j):
-        rows = pl.ds(pl.multiple_of(j * 2 * tok, 2 * tok), 2 * tok)
-
-        def tile(t, carry):
-            cols = pl.ds(pl.multiple_of(t * 512, 512), 512)
-            parts_m[rows, cols] = mm(mid[rows, :], wd[:, cols], NN).astype(BF16)
-            total = None
-            for e in range(exp_dev):
-                for w, base in ((wg, 0), (wu, exp_dev)):
-                    term = mm(dgu[rows, pl.ds((base + e) * ff, ff)], w[e, cols, :], NT)
-                    total = term if total is None else total + term
-            parts_r[rows, cols] = total.astype(BF16)
-            return carry
-
-        lax.fori_loop(0, model // 512, tile, 0)
-
     def pair(j, carry):
-        @pl.when(j == 3)
-        def _():
-            for side in range(2):
-                take_packed(side, 1)
-
-        stage_one(j)
-
-        @pl.when(j == 0)
-        def _():
-            for side in range(2):
-                late(side, 0, 1).wait_recv()
-                late(side, 1, 1).start()
-
-        @pl.when(j == 1)
+        base = pl.multiple_of(j * 2 * tok, 2 * tok)
+
+        @pl.when(j == 2)
         def _():
             for part in range(2):
                 for side in range(2):
                     late(side, 1, part).wait_recv()
             for side in range(2):
-                send_packed(side, 1)
+                pack_last(side, 1)
+                packed_copy(side, 1).start()
+
+        @pl.when(j == 3)
+        def _():
+            for side in range(2):
+                take_packed(side, 0)
+            stage_one(tok, tok)
+            stage_two(tok, tok, tok)
             return_first(0)
-
-        stage_two(j)
+            for side in range(2):
+                take_packed(side, 1)
+
+        stage_one(base, 2 * tok)
+
+        @pl.when(j < 3)
+        def _():
+            stage_two(base, base, 2 * tok)
+
         return carry
 
-    lax.fori_loop(0, 4, pair, 0)
+    lax.fori_loop(1, 4, pair, 0)
+    stage_two(7 * tok, 6 * tok, tok)
     return_first(1)
+    stage_two(6 * tok, 7 * tok, tok)
 
     lane = lax.broadcasted_iota(jnp.int32, (tok, 128), 1)
     stacked = jnp.zeros((tok, 128), F32)
@@ -457,7 +465,7 @@
 
                 def unpack(t, carry):
                     rows, cols = pl.ds(base, tok), pl.ds(pl.multiple_of(t * 512, 512), 512)
-                    got = mm(pick[which], landed[side, index - 2, pl.ds(0, few), cols], TN)
+                    got = mm(pick[which], landed_few[side, index - 2, :, cols], TN)
                     buf[rows, cols] = (buf[rows, cols].astype(F32) + got).astype(BF16)
                     return carry
 
@@ -467,7 +475,7 @@
 
             def add(t, carry):
                 rows = pl.ds(pl.multiple_of(base + t * 32, 32), 32)
-                got = landed[side, index - 2, pl.ds(pl.multiple_of(t * 32, 32), 32), :]
+                got = landed[side, index - 4, pl.ds(pl.multiple_of(t * 32, 32), 32), :]
                 buf[rows, :] = (buf[rows, :].astype(F32) + got.astype(F32)).astype(BF16)
                 return carry
 
@@ -530,8 +538,8 @@
             dwgu[own, :].astype(F32) + pr_gu[1, rows, :].astype(F32) + xr_gu[rows, :].astype(F32)
         ).astype(BF16)
         for e in range(exp_dev):
-            ogate_ref[e, rows, :] = total[:, e * ff : (e + 1) * ff]
-            oup_ref[e, rows, :] = total[:, (exp_dev + e) * ff : (exp_dev + e + 1) * ff]
+            sgate[e, rows, :] = total[:, e * ff : (e + 1) * ff]
+            sup[e, rows, :] = total[:, (exp_dev + e) * ff : (exp_dev + e + 1) * ff]
         return carry
 
     lax.fori_loop(0, quarter // 32, final_gu, 0)
@@ -539,7 +547,7 @@
         def final_down(t, carry):
             at = pl.multiple_of(t * 32, 32)
             rows = pl.ds(pl.multiple_of(e * ff + at, 32), 32)
-            odown_ref[e, pl.ds(at, 32), :] = (
+            sdown[e, pl.ds(at, 32), :] = (
                 dwd[near_own, rows, :].astype(F32)
                 + pr_d[1, rows, :].astype(F32)
                 + xr_d[rows, :].astype(F32)
@@ -547,6 +555,14 @@
             return carry
 
         lax.fori_loop(0, ff // 32, final_down, 0)
+
+    leaving = [
+        pltpu.make_async_copy(sgate, ogate_ref, local_sem.at[1]),
+        pltpu.make_async_copy(sup, oup_ref, local_sem.at[2]),
+        pltpu.make_async_copy(sdown, odown_ref, local_sem.at[3]),
+    ]
+    for copy in leaving:
+        copy.start()
 
     for index in (5, 6):
         for side in range(2):
@@ -560,7 +576,7 @@
                 rows = pl.ds(pl.multiple_of(t * 32, 32), 32)
                 so_far = buf if index == 5 else out
                 out[rows, :] = (
-                    so_far[rows, :].astype(F32) + landed[side, index, rows, :].astype(F32)
+                    so_far[rows, :].astype(F32) + landed[side, index - 2, rows, :].astype(F32)
                 ).astype(BF16)
                 return carry
 
@@ -581,6 +597,8 @@
         dots_copy(k).wait_send()
     for case in range(4):
         relay_gates(case).wait_send()
+    for copy in leaving:
+        copy.wait()
     for copy in far_swap + near_swap + far_send:
         copy.wait_send()
 
@@ -621,7 +639,7 @@
             jax.ShapeDtypeStruct((exp_dev, ff, quarter), BF16),
         ),
         in_specs=[hbm] * 5 + [vmem] * 2,
-        out_specs=[vmem] * 6,
+        out_specs=[vmem] * 3 + [hbm] * 3,
         scratch_shapes=[
             pltpu.VMEM((rows, model), BF16),
             pltpu.VMEM((rows, model), BF16),
@@ -634,7 +652,8 @@
             pltpu.VMEM((rows, mids), BF16),
             pltpu.VMEM((model, 2 * mids), BF16),
             pltpu.VMEM((dps, mids, quarter), BF16),
-            pltpu.VMEM((2, 7, tok, model), BF16),
+            pltpu.VMEM((2, 5, tok, model), BF16),
+            pltpu.VMEM((2, 2, few, model), BF16),
             pltpu.VMEM((2, quarter, 2 * mids), BF16),
             pltpu.VMEM((2, mids, quarter), BF16),
             pltpu.VMEM((quarter, 2 * mids), BF16),
@@ -647,6 +666,9 @@
             pltpu.VMEM((owners, 8, 128), F32),
             pltpu.VMEM((7, few, tok), BF16),
             pltpu.VMEM((2, 2, few, model), BF16),
+            pltpu.VMEM((exp_dev, quarter, ff), BF16),
+            pltpu.VMEM((exp_dev, quarter, ff), BF16),
+            pltpu.VMEM((exp_dev, ff, quarter), BF16),
             dma((5,)),
             dma((2, 14)),
             dma((2, 14)),

time: 171 us -> 166 us (0.971)
  Pallas kernels: 171 us -> 165 us
    pallas_call x1, Pallas kernels: 168 us -> 163 us  [local(): pl.pallas_call(layer_kernel, out_shape=(jax.ShapeDtypeStruct((tok, model)...]
where the time goes in v3:
time: 166 us
  Pallas kernels  165 us (99%)
    pallas_call x1, Pallas kernels, local(): pl.pallas_call(layer_kernel, out_shape=(jax.ShapeDtypeStruct((tok, model)...  163 us

profile of v3, /device:TPU:0, one launch (start us, length us, event | category | flops | bytes accessed | tf_op | source)
XLA Modules:
  0.0 166.3 jit_solution(18299293783267844855)
XLA Ops:
  0.6 162.5 %moe_layer.1 = (bf16[128,2048]{1,0:T(8,128)(2,1)}, bf16[128,2048]{1,0:T(8,128)(2,1)}, f32[4,128]{1,0:T(4,128)}, bf16[2,512,384]{2,1,0:T(8,128)(2,1)}, bf16[2,512...) custom-call(bf16[128,2048]{1,0:T(8,128)(2,1)} %tok_in.1, bf16[128,2048]{1,0:T(8,128)(2,1)} %grad_in.1, ...), custom_call_target="tpu_custom_call" | custom-call | tf_op jit(solution)/shard_map/moe_layer/pallas_call | solution.py:631
  163.2 3.0 %hand_over.1 = (bf16[128,2048]{1,0:T(8,128)(2,1)}, bf16[128,2048]{1,0:T(8,128)(2,1)}, f32[4,128]{1,0:T(4,128)}, bf16[2,512,384]{2,1,0:T(8,128)(2,1)}, bf16[2,512...) custom-call(bf16[128,2048]{1,0:T(8,128)(2,1)} %get-tuple-element.18.refs_0_, ...), custom_call_target="tpu_custom_call" | custom-call | tf_op jit(solution)/shard_map/hand_over/pallas_call | solution.py:687

commit v4 on v3

--- a/solution.py
+++ b/solution.py
@@ -419,6 +419,7 @@
 
         lax.fori_loop(0, quarter // 256, tile, 0)
 
+    def down_grads(piece):
         def tile_down(t, carry):
             at = pl.multiple_of(t * 256, 256)
             dwd[piece, pl.ds(at, 256), :] = mm(
@@ -483,12 +484,10 @@
             back_copy(side, index).start()
 
     weight_grads(far_partner)
-    for copy in far_swap:
-        copy.start()
+    far_swap[0].start()
     return_step(2)
     weight_grads(far_own)
-    for copy in far_swap:
-        copy.wait_recv()
+    far_swap[0].wait_recv()
 
     def add_far(t, carry):
         rows = pl.ds(pl.multiple_of(far_own * quarter + t * 32, 32), 32)
@@ -498,6 +497,10 @@
 
     lax.fori_loop(0, quarter // 32, add_far, 0)
     far_send[0].start()
+    down_grads(far_partner)
+    far_swap[1].start()
+    down_grads(far_own)
+    far_swap[1].wait_recv()
 
     def add_far_down(t, carry):
         rows = pl.ds(pl.multiple_of(t * 32, 32), 32)
@@ -510,10 +513,12 @@
     far_send[1].start()
     return_step(3)
     weight_grads(near_partner)
+    down_grads(near_partner)
     for copy in near_swap:
         copy.start()
     return_step(4)
     weight_grads(near_own)
+    down_grads(near_own)
     return_step(5)
 
     own_dots.wait()
@@ -528,8 +533,7 @@
 
     for copy in near_swap:
         copy.wait_recv()
-    for copy in far_send:
-        copy.wait_recv()
+    far_send[0].wait_recv()
 
     def final_gu(t, carry):
         rows = pl.ds(pl.multiple_of(t * 32, 32), 32)
@@ -542,7 +546,34 @@
             sup[e, rows, :] = total[:, (exp_dev + e) * ff : (exp_dev + e + 1) * ff]
         return carry
 
+    def close_step(index):
+        for side in range(2):
+            back_copy(side, index).wait_recv()
+        kind = orders[0][index][0]
+        other = orders[1][index][0]
+        for side, name in ((0, kind), (1, other)):
+            buf, out = bufs[name], {"m": mixed_ref, "r": dtok_ref}[name]
+
+            def close(t, carry):
+                rows = pl.ds(pl.multiple_of(t * 32, 32), 32)
+                so_far = buf if index == 5 else out
+                out[rows, :] = (
+                    so_far[rows, :].astype(F32) + landed[side, index - 2, rows, :].astype(F32)
+                ).astype(BF16)
+                return carry
+
+            lax.fori_loop(0, tok // 32, close, 0)
+
     lax.fori_loop(0, quarter // 32, final_gu, 0)
+    leaving = [
+        pltpu.make_async_copy(sgate, ogate_ref, local_sem.at[1]),
+        pltpu.make_async_copy(sup, oup_ref, local_sem.at[2]),
+        pltpu.make_async_copy(sdown, odown_ref, local_sem.at[3]),
+    ]
+    leaving[0].start()
+    leaving[1].start()
+    close_step(5)
+    far_send[1].wait_recv()
     for e in range(exp_dev):
         def final_down(t, carry):
             at = pl.multiple_of(t * 32, 32)
@@ -556,31 +587,8 @@
 
         lax.fori_loop(0, ff // 32, final_down, 0)
 
-    leaving = [
-        pltpu.make_async_copy(sgate, ogate_ref, local_sem.at[1]),
-        pltpu.make_async_copy(sup, oup_ref, local_sem.at[2]),
-        pltpu.make_async_copy(sdown, odown_ref, local_sem.at[3]),
-    ]
-    for copy in leaving:
-        copy.start()
-
-    for index in (5, 6):
-        for side in range(2):
-            back_copy(side, index).wait_recv()
-        kind = orders[0][index][0]
-        other = orders[1][index][0]
-        for side, name in ((0, kind), (1, other)):
-            buf, out = bufs[name], {"m": mixed_ref, "r": dtok_ref}[name]
-
-            def close(t, carry):
-                rows = pl.ds(pl.multiple_of(t * 32, 32), 32)
-                so_far = buf if index == 5 else out
-                out[rows, :] = (
-                    so_far[rows, :].astype(F32) + landed[side, index - 2, rows, :].astype(F32)
-                ).astype(BF16)
-                return carry
-
-            lax.fori_loop(0, tok // 32, close, 0)
+    leaving[2].start()
+    close_step(6)
 
     for side in range(2):
         for index in range(6):

time: 166 us -> 165 us (level)
  no operation moved by 1% of the time
where the time goes in v4:
time: 165 us
  Pallas kernels  164 us (99%)
    pallas_call x1, Pallas kernels, local(): pl.pallas_call(layer_kernel, out_shape=(jax.ShapeDtypeStruct((tok, model)...  161 us

profile of v4, /device:TPU:0, one launch (start us, length us, event | category | flops | bytes accessed | tf_op | source)
XLA Modules:
  0.0 164.9 jit_solution(18362674109590645253)
XLA Ops:
  0.6 161.2 %moe_layer.1 = (bf16[128,2048]{1,0:T(8,128)(2,1)}, bf16[128,2048]{1,0:T(8,128)(2,1)}, f32[4,128]{1,0:T(4,128)}, bf16[2,512,384]{2,1,0:T(8,128)(2,1)}, bf16[2,512...) custom-call(bf16[128,2048]{1,0:T(8,128)(2,1)} %tok_in.1, bf16[128,2048]{1,0:T(8,128)(2,1)} %grad_in.1, ...), custom_call_target="tpu_custom_call" | custom-call | tf_op jit(solution)/shard_map/moe_layer/pallas_call | solution.py:639
  161.8 3.0 %hand_over.1 = (bf16[128,2048]{1,0:T(8,128)(2,1)}, bf16[128,2048]{1,0:T(8,128)(2,1)}, f32[4,128]{1,0:T(4,128)}, bf16[2,512,384]{2,1,0:T(8,128)(2,1)}, bf16[2,512...) custom-call(bf16[128,2048]{1,0:T(8,128)(2,1)} %get-tuple-element.18.refs_0_, ...), custom_call_target="tpu_custom_call" | custom-call | tf_op jit(solution)/shard_map/hand_over/pallas_call | solution.py:695
